TPU v7x, 32 devices: a whole 2x2x4 slice. The times are simulated.
32 devices in a mesh: seq: 8 (over y, x, core), dp: 4 (over z).
Axes of the slice: x: 2, y: 2, z: 4, core: 2. Of those that a mesh axis runs over, the one named last changes fastest.
Arguments:
- history: bfloat16 [9, 1024, 4096], P(None, 'seq', 'dp'), may hold values from -6 to 6
- cotangent: bfloat16 [1024, 4096], P('seq', 'dp'), may hold values from -6 to 6
- bucket_len: int32 [4, 8, 2], P('dp', 'seq'), may hold values from 32 to 96, as said below
- valid_len: int32 [4, 8, 2], P('dp', 'seq'), may hold values from 1 to 96, as said below
- gen_gain: float32 [1024], replicated, may hold values from 0.25 to 1.75
- gen_in: bfloat16 [1024, 40], replicated, may hold values from -0.1875 to 0.1875
- gen_out: float32 [40, 4, 9], replicated, may hold values from -1 to 1
- gen_bias: float32 [4, 9], replicated, may hold values from -3 to 3
- norm_gain: float32 [2, 1024], replicated, may hold values from 0.25 to 1.75
- norm_bias: float32 [2, 1024], replicated, may hold values from -2 to 2
- w_in: bfloat16 [1024, 7, 1024], P('seq'), may hold values from -0.1875 to 0.1875
- in_bias: float32 [7, 1024], replicated, may hold values from -2 to 2
- w_out: bfloat16 [1024, 1024], P('seq'), may hold values from -0.75 to 0.75
- w_down: bfloat16 [1024, 4096], P('seq'), may hold values from -0.09375 to 0.09375
- out_bias: float32 [1024], replicated, may hold values from -2 to 2
Outputs:
- new_state: bfloat16 [1024, 4096], P('seq', 'dp')
- history_grad: bfloat16 [9, 1024, 4096], P(None, 'seq', 'dp')
- mix_mean: float32 [4, 9], replicated
- mix_var: float32 [4, 9], replicated
- gen_gain_grad: float32 [1024], replicated
- gen_in_grad: float32 [1024, 40], replicated
- gen_out_grad: float32 [40, 4, 9], replicated
- gen_bias_grad: float32 [4, 9], replicated
- norm_gain_grad: float32 [2, 1024], replicated
- norm_bias_grad: float32 [2, 1024], replicated
- w_in_grad: float32 [1024, 7, 1024], P('seq')
- in_bias_grad: float32 [7, 1024], replicated
- w_out_grad: float32 [1024, 1024], P('seq')
- w_down_grad: float32 [1024, 4096], P('seq')
- out_bias_grad: float32 [1024], replicated
Inputs may be any that keep to these rules, and one draw needn't show every extreme that they name: `bucket_len`: the two buckets of one token block together hold 128 tokens. Each bucket's valid tokens are its first valid_len tokens, at least one and at most the bucket's length.
All inputs are finite; a program needn't handle non-finite values.
Results may differ from a plain program's by a relative error of at most 0.015.
Values may be sent and summed in bfloat16 or wider, within the bound.
A program may use at most 256 MiB of HBM per device.

v0:
```python
import math
import jax
import jax.numpy as jnp
from jax import lax
from jax.sharding import PartitionSpec as P

HEADS = 16
HEAD_DIM = 64
ROT = 16
ln_eps = 1e-05
rms_eps = 1e-06
masked_score = -1e30
highest = lax.Precision.HIGHEST


def gelu_exact(values):
    return jax.nn.gelu(values, approximate=False)


def rotary_tables(position):
    freq_index = jnp.arange(ROT // 2, dtype=jnp.float32)
    inverse_freq = jnp.exp(freq_index * (-2.0 * math.log(10000.0) / ROT))
    angles = position.astype(jnp.float32)[:, None] * inverse_freq[None, :]
    return (jnp.cos(angles), jnp.sin(angles))


def rotate(values, cosine, sine):
    half = ROT // 2
    former = values[..., :half]
    latter = values[..., half:ROT]
    cos_heads = cosine[:, None, :]
    sin_heads = sine[:, None, :]
    return jnp.concatenate(
        [
            former * cos_heads - latter * sin_heads,
            latter * cos_heads + former * sin_heads,
            values[..., ROT:],
        ],
        axis=-1,
    )


def token_layout(lengths, counts, tokens):
    index = jnp.arange(tokens, dtype=jnp.int32)
    second = index >= lengths[0]
    position = index - jnp.where(second, lengths[0], 0)
    valid = position < jnp.where(second, counts[1], counts[0])
    return (second, position, valid)


def normalize(streams):
    centre = jnp.mean(streams, axis=-1, keepdims=True)
    centred = streams - centre
    inverse = lax.rsqrt(jnp.mean(centred * centred, axis=-1, keepdims=True) + ln_eps)
    return (centred * inverse, inverse)


def normalize_back(grad_scaled, scaled, inverse):
    mean_grad = jnp.mean(grad_scaled, axis=-1, keepdims=True)
    mean_along = jnp.mean(grad_scaled * scaled, axis=-1, keepdims=True)
    return inverse * (grad_scaled - mean_grad - scaled * mean_along)


def per_device(
    history,
    cotangent,
    bucket_len,
    valid_len,
    gen_gain,
    gen_in,
    gen_out,
    gen_bias,
    norm_gain,
    norm_bias,
    w_in,
    in_bias,
    w_out,
    w_down,
    out_bias,
):
    states = history.shape[0]
    stacked = jnp.concatenate([history, cotangent[None]], axis=0)
    arrived = lax.all_to_all(stacked, "seq", split_axis=2, concat_axis=1, tiled=True)
    arrived_rows = jnp.swapaxes(arrived, 1, 2)
    hist_local = arrived_rows[:states]
    cot_local = arrived_rows[states]
    tokens = hist_local.shape[1]
    width = hist_local.shape[2]
    second, position, valid = token_layout(bucket_len.reshape(2), valid_len.reshape(2), tokens)
    valid_float = valid.astype(jnp.float32)
    last = hist_local[states - 1].astype(jnp.float32)
    rms = lax.rsqrt(jnp.mean(last * last, axis=-1, keepdims=True) + rms_eps)
    gen_normed = (last * rms * gen_gain).astype(jnp.bfloat16)
    gen_pre = jnp.dot(gen_normed, gen_in, preferred_element_type=jnp.float32)
    gen_hidden, gen_pull = jax.vjp(gelu_exact, gen_pre)
    mixing = jnp.einsum("th,hsj->tsj", gen_hidden, gen_out, precision=highest) + gen_bias
    weighted = mixing * valid_float[:, None, None]
    stat_sums = jnp.sum(weighted, axis=0)
    stat_squares = jnp.sum(weighted * mixing, axis=0)
    stat_count = jnp.sum(valid_float)
    streams = mixing[:, :, 0].T[:, :, None] * hist_local[0]
    for state in range(1, states):
        streams = streams + mixing[:, :, state].T[:, :, None] * hist_local[state]
    scaled, inverse = normalize(streams)
    normed_attn = (scaled[:3] * norm_gain[0] + norm_bias[0]).astype(jnp.bfloat16)
    normed_mlp = (scaled[3] * norm_gain[1] + norm_bias[1]).astype(jnp.bfloat16)
    piece = lax.all_gather(w_in, "seq", axis=0, tiled=True)
    attn_part = jnp.einsum(
        "stk,nsk->stn", normed_attn, piece[:, :3], preferred_element_type=jnp.float32
    )
    mlp_part = jnp.einsum(
        "tk,njk->jtn", normed_mlp, piece[:, 3:], preferred_element_type=jnp.float32
    )
    projected = jnp.concatenate([attn_part, mlp_part], axis=0) + in_bias[:, None, :]
    cosine, sine = rotary_tables(position)
    heads_shape = (tokens, HEADS, HEAD_DIM)
    queries = (rotate(projected[0].reshape(heads_shape), cosine, sine) * HEAD_DIM ** (-0.5)).astype(
        jnp.bfloat16
    )
    keys = rotate(projected[1].reshape(heads_shape), cosine, sine).astype(jnp.bfloat16)
    values = projected[2].reshape(heads_shape).astype(jnp.bfloat16)
    index = jnp.arange(tokens, dtype=jnp.int32)
    allowed = (
        (second[:, None] == second[None, :]) & (index[None, :] <= index[:, None]) & valid[None, :]
    )
    scores = jnp.einsum("qhd,khd->hqk", queries, keys, preferred_element_type=jnp.float32)
    scores = jnp.where(allowed[None], scores, masked_score)
    top = jnp.max(scores, axis=-1, keepdims=True)
    weights = jnp.exp(scores - top)
    weight_total = jnp.sum(weights, axis=-1, keepdims=True)
    log_total = top + jnp.log(weight_total)
    probs_low = (weights / weight_total).astype(jnp.bfloat16)
    attended = jnp.einsum("hqk,khd->qhd", probs_low, values, preferred_element_type=jnp.float32)
    attn_low = attended.reshape(tokens, width).astype(jnp.bfloat16)
    gelu_up, up_pull = jax.vjp(gelu_exact, projected[3:])
    gelu_low = gelu_up.astype(jnp.bfloat16)
    grad_out_low = jnp.where(valid[:, None], cot_local, jnp.zeros_like(cot_local))
    piece_out, piece_down = lax.all_gather((w_out, w_down), "seq", axis=0, tiled=True)
    down_part = piece_down.reshape(piece_down.shape[0], 4, width)
    result = jnp.einsum("tk,nk->tn", attn_low, piece_out, preferred_element_type=jnp.float32)
    branch = result + jnp.einsum(
        "jtk,njk->tn", gelu_low, down_part, preferred_element_type=jnp.float32
    )
    new_local = (streams[3] + branch + out_bias).astype(jnp.bfloat16)
    piece_out = lax.all_gather(w_out, "seq", axis=0, tiled=True)
    piece_down = lax.all_gather(w_down, "seq", axis=0, tiled=True)
    count = piece_out.shape[0]
    part = grad_out_low
    attn_add = jnp.einsum("tn,nk->tk", part, piece_out, preferred_element_type=jnp.float32)
    gelu_add = jnp.einsum(
        "tn,njk->jtk", part, piece_down.reshape(count, 4, width), preferred_element_type=jnp.float32
    )
    grad_attn = attn_add
    part = grad_out_low
    term_out = jnp.einsum("tn,tk->nk", part, attn_low, preferred_element_type=jnp.float32)
    term_down = jnp.einsum(
        "tn,jtk->njk", part, gelu_low, preferred_element_type=jnp.float32
    ).reshape(lax.axis_size("seq") * w_out.shape[0], 4 * width)
    out_grads = lax.psum_scatter(
        jnp.concatenate([term_out, term_down], axis=1).astype(jnp.bfloat16),
        "seq",
        scatter_dimension=0,
        tiled=True,
    )
    out_bias_grad = jnp.sum(grad_out_low.astype(jnp.float32), axis=0)
    grad_attended = grad_attn.astype(jnp.bfloat16).reshape(heads_shape)
    rescored = jnp.einsum("qhd,khd->hqk", queries, keys, preferred_element_type=jnp.float32)
    probs = jnp.where(allowed[None], jnp.exp(rescored - log_total), 0.0)
    grad_values = jnp.einsum(
        "hqk,qhd->khd",
        probs.astype(jnp.bfloat16),
        grad_attended,
        preferred_element_type=jnp.float32,
    )
    grad_probs = jnp.einsum(
        "qhd,khd->hqk", grad_attended, values, preferred_element_type=jnp.float32
    )
    grad_scores = (
        probs * (grad_probs - jnp.sum(probs * grad_probs, axis=-1, keepdims=True))
    ).astype(jnp.bfloat16)
    grad_queries = jnp.einsum(
        "hqk,khd->qhd", grad_scores, keys, preferred_element_type=jnp.float32
    ) * HEAD_DIM ** (-0.5)
    grad_keys = jnp.einsum("hqk,qhd->khd", grad_scores, queries, preferred_element_type=jnp.float32)
    grad_up = up_pull(gelu_add)[0]
    grad_proj = jnp.concatenate(
        [
            rotate(grad_queries, cosine, -sine).reshape(1, tokens, width),
            rotate(grad_keys, cosine, -sine).reshape(1, tokens, width),
            grad_values.reshape(1, tokens, width),
            grad_up,
        ],
        axis=0,
    )
    in_bias_grad = jnp.sum(grad_proj, axis=1)
    grad_proj_low = grad_proj.astype(jnp.bfloat16)
    piece = lax.all_gather(w_in, "seq", axis=0, tiled=True)
    part = grad_proj_low
    attn_add = jnp.einsum(
        "stn,nsk->stk", part[:3], piece[:, :3], preferred_element_type=jnp.float32
    )
    mlp_add = jnp.einsum("jtn,njk->tk", part[3:], piece[:, 3:], preferred_element_type=jnp.float32)
    part = grad_proj_low
    attn_term = jnp.einsum(
        "stn,stk->nsk", part[:3], normed_attn, preferred_element_type=jnp.float32
    )
    mlp_term = jnp.einsum("jtn,tk->njk", part[3:], normed_mlp, preferred_element_type=jnp.float32)
    in_grads = lax.psum_scatter(
        jnp.concatenate([attn_term, mlp_term], axis=1).astype(jnp.bfloat16),
        "seq",
        scatter_dimension=0,
        tiled=True,
    )
    norm_gain_grad = jnp.stack(
        [jnp.sum(attn_add * scaled[:3], axis=(0, 1)), jnp.sum(mlp_add * scaled[3], axis=0)]
    )
    norm_bias_grad = jnp.stack([jnp.sum(attn_add, axis=(0, 1)), jnp.sum(mlp_add, axis=0)])
    grad_attn_streams = normalize_back(attn_add * norm_gain[0], scaled[:3], inverse[:3])
    grad_mlp_stream = normalize_back(
        mlp_add * norm_gain[1], scaled[3], inverse[3]
    ) + grad_out_low.astype(jnp.float32)
    grad_streams = jnp.concatenate([grad_attn_streams, grad_mlp_stream[None]], axis=0)
    grad_mixing = jnp.stack(
        [
            jnp.einsum(
                "std,td->ts", grad_streams, hist_local[state].astype(jnp.float32), precision=highest
            )
            for state in range(states)
        ],
        axis=-1,
    )
    hist_terms = [
        jnp.einsum("ts,std->td", mixing[:, :, state], grad_streams, precision=highest)
        for state in range(states)
    ]
    gen_bias_grad = jnp.sum(grad_mixing, axis=0)
    gen_out_grad = jnp.einsum("th,tsj->hsj", gen_hidden, grad_mixing, precision=highest)
    grad_hidden = jnp.einsum("tsj,hsj->th", grad_mixing, gen_out, precision=highest)
    grad_pre_low = gen_pull(grad_hidden)[0].astype(jnp.bfloat16)
    gen_in_grad = jnp.einsum(
        "tk,th->kh", gen_normed, grad_pre_low, preferred_element_type=jnp.float32
    )
    grad_gen = jnp.einsum("th,kh->tk", grad_pre_low, gen_in, preferred_element_type=jnp.float32)
    gen_gain_grad = jnp.sum(grad_gen * last * rms, axis=0)
    gained = grad_gen * gen_gain
    grad_last = rms * gained - last * (rms * rms * rms) * jnp.mean(
        gained * last, axis=-1, keepdims=True
    )
    hist_stack = jnp.stack(hist_terms[: states - 1] + [hist_terms[states - 1] + grad_last]).astype(
        jnp.bfloat16
    )
    departing = jnp.swapaxes(jnp.concatenate([new_local[None], hist_stack], axis=0), 1, 2)
    returned = lax.all_to_all(departing, "seq", split_axis=1, concat_axis=2, tiled=True)
    w_in_grad, out_total = (
        lax.psum(in_grads, "dp").astype(jnp.float32),
        lax.psum(out_grads, "dp").astype(jnp.float32),
    )
    w_out_grad = out_total[:, :width]
    w_down_grad = out_total[:, width:]
    joined = lax.psum(
        (
            gen_gain_grad,
            gen_in_grad,
            gen_out_grad,
            gen_bias_grad,
            norm_gain_grad,
            norm_bias_grad,
            in_bias_grad,
            out_bias_grad,
            stat_sums,
            stat_squares,
            stat_count,
        ),
        ("seq", "dp"),
    )
    small_totals = joined[:8]
    stat_totals = joined[8:]
    mix_mean = stat_totals[0] / stat_totals[2]
    mix_var = stat_totals[1] / stat_totals[2] - mix_mean * mix_mean
    return (
        returned[0],
        returned[1:],
        mix_mean,
        mix_var,
        small_totals[0],
        small_totals[1],
        small_totals[2],
        small_totals[3],
        small_totals[4],
        small_totals[5],
        w_in_grad,
        small_totals[6],
        w_out_grad,
        w_down_grad,
        small_totals[7],
    )


def solution(mesh):
    in_specs = (
        P(None, "seq", "dp"),
        P("seq", "dp"),
        P("dp", "seq", None),
        P("dp", "seq", None),
        P(),
        P(),
        P(),
        P(),
        P(),
        P(),
        P("seq", None, None),
        P(),
        P("seq", None),
        P("seq", None),
        P(),
    )
    out_specs = (
        P("seq", "dp"),
        P(None, "seq", "dp"),
        P(),
        P(),
        P(),
        P(),
        P(),
        P(),
        P(),
        P(),
        P("seq", None, None),
        P(),
        P("seq", None),
        P("seq", None),
        P(),
    )
    return jax.shard_map(
        per_device, mesh=mesh, in_specs=in_specs, out_specs=out_specs, check_vma=False
    )
```

profile of v0, /device:TPU:8, one launch (start us, length us, event | category | flops | bytes accessed | tf_op | source)
XLA Modules:
  0.0 705.1 jit_solution(17909491425658481265)
XLA Ops:
  11.4 7.4 %copy.110 = bf16[9,128,1024]{1,0,2:T(8,128)(2,1)} copy(bf16[9,128,1024]{2,1,0:T(8,128)(2,1)S(1)} %copy-done.17) | data formatting | bytes 4718592 | tf_op args[0]
  18.8 6.1 pad_maximum_fusion.2
  33.1 64.4 %all-to-all-done = bf16[10,128,1024]{1,0,2:T(8,128)(2,1)} async-done(((bf16[10,128,1024]{1,0,2:T(8,128)(2,1)}), bf16[10,128,1024]{1,0,2:T(8,128)(2,1)}, u32[]{:S(2)}, u32[]{:S(2)}) %all-to-all-start) | async-done | bytes 2621472 | tf_op jit(solution)/shard_map/all_to_all | solution.py:83
  97.5 5.4 copy.298
  117.8 33.5 %all-gather.4.cloned.1.call-done = bf16[1024,7,1024]{2,0,1:T(8,128)(2,1)} async-done(((bf16[128,7,1024]{2,0,1:T(8,128)(2,1)}), bf16[1024,7,1024]{2,0,1:T(8,128)(2,1)}) %all-gather.4.cloned.1.call-update) | async-done | bytes 14680080 | tf_op jit(solution)/shard_map/all_gather | solution.py:107
  151.3 5.0 fusion.6
  156.3 6.3 fusion.22
  184.9 7.3 %multiply_convert_fusion = (bf16[4,128,1024]{2,1,0:T(8,128)(2,1)}, f32[4,128,1024]{2,1,0:T(8,128)}) fusion(f32[7,128,1024]{2,1,0:T(8,128)} %copy-done.3), kind=kLoop, calls=%fused_computation.30 | loop fusion | flops 34078720 | bytes 5242880 | tf_op jit(solution)/shard_map/convert_element_type | solution.py:136
  192.2 16.9 %all-gather.8.cloned.1.call-done = bf16[1024,4096]{0,1:T(8,128)(2,1)} async-done(((bf16[128,4096]{0,1:T(8,128)(2,1)}), bf16[1024,4096]{0,1:T(8,128)(2,1)}) %all-gather.8.cloned.1.call-update) | async-done | bytes 8388624 | tf_op jit(solution)/shard_map/all_gather | solution.py:138
  209.1 8.0 %fusion.15 = f32[4,128,1024]{2,1,0:T(8,128)S(1)} fusion(f32[4,128,1024]{2,1,0:T(8,128)} %get-tuple-element.106, f32[7,128,1024]{2,1,0:T(8,128)} %copy-done.3, bf16[1024,4,1024]{0,2,1:T(8,128)(2,1)} %bitcast.374, pred[128]{0:T(512)(128)(4,1)S(1)} %copy-done.57, bf16[10,128,1024]{2,1,0:T(8,128)(2,1)} %bitcast.365), kind=kOutput, calls=%fused_computation.28 | convolution fusion | flops 1080688640 | bytes 14942336 | tf_op jit(solution)/shard_map/tn,njk->jtk/dot_general | solution.py:150
  223.3 8.3 %pad_maximum_fusion = bf16[1024,7,1024]{0,2,1:T(8,128)(2,1)} fusion(bf16[1024,4,1024]{0,2,1:T(8,128)(2,1)S(1)} %convert_bitcast_fusion, bf16[1024,3,1024]{0,2,1:T(8,128)(2,1)S(1)} %convert_bitcast_fusion.1), kind=kLoop, calls=%fused_computation | loop fusion | flops 7340032 | bytes 29360128 | tf_op jit(solution)/shard_map/concatenate | solution.py:209
  231.6 18.5 %copy.186 = bf16[1024,7168]{1,0:T(8,128)(2,1)} copy(bf16[1024,7168]{0,1:T(8,128)(2,1)} %bitcast.360) | data formatting | bytes 29360128
  264.6 6.3 pad_maximum_fusion.1
  278.1 5.9 multiply_reduce_fusion.5
  284.0 5.0 multiply_reduce_fusion.1
  301.2 5.0 fusion.64
  317.2 5.2 fusion.58
  333.9 5.6 fusion.52
  343.5 5.2 fusion.154
  348.8 4.9 convolution_bitcast_fusion.1
  388.6 51.7 %reduce-scatter.5.cloned.1.call-done = bf16[128,5120]{1,0:T(8,128)(2,1)} async-done(((bf16[1024,5120]{1,0:T(8,128)(2,1)}), bf16[128,5120]{1,0:T(8,128)(2,1)}) %reduce-scatter.5.cloned.1.call-update) | async-done | bytes 1310736 | tf_op jit(solution)/shard_map/reduce_scatter | solution.py:159
  457.2 6.8 copy.129
  472.8 81.4 %all-reduce = (f32[4,9]{1,0:T(4,128)S(1)}, f32[]{:T(128)}, f32[4,9]{1,0:T(4,128)S(1)}, f32[1024]{0:T(1024)}, f32[40,4,9]{0,2,1:T(8,128)S(1)}, /*index=5*/f32[4,9...) all-reduce(f32[4,9]{1,0:T(4,128)S(1)} %copy-done.85, ...), channel_id=1, replica_groups=mesh['seq'=8,'dp'=4] {'seq','dp'}, use_global_device_ids=true, to_apply=%region_12.13 | all-reduce | flops 14861 | bytes 118888 | tf_op jit(solution)/shard_map/psum | solution.py:260
  574.8 121.5 %all-reduce.5.cloned.1.call-done = f32[1024,40]{0,1:T(8,128)} async-done(((f32[1024,40]{0,1:T(8,128)}), f32[1024,40]{0,1:T(8,128)}) %all-reduce.5.cloned.1.call-update) | async-done | bytes 163856 | tf_op jit(solution)/shard_map/psum | solution.py:260
  (353 shorter events, 197.9 us)
Async XLA Ops:
  7.2 101.2 %copy-start = (bf16[1024,40]{0,1:T(8,128)(2,1)S(1)}, bf16[1024,40]{0,1:T(8,128)(2,1)}, u32[]{:S(2)}) copy-start(bf16[1024,40]{0,1:T(8,128)(2,1)} %param.20) | copy-start | bytes 245764
  7.2 108.2 %all-gather.6.cloned.1.call-start = ((), (), s32[]{:S(2)}) async-start(), calls=%async_computation.5 | async-start | bytes 2359296 | tf_op jit(solution)/shard_map/all_gather | solution.py:138
  7.9 143.4 %all-gather.4.cloned.1.call-start = ((), (), s32[]{:S(2)}) async-start(), calls=%async_computation.4 | async-start | bytes 16515072 | tf_op jit(solution)/shard_map/all_gather | solution.py:107
  8.7 200.4 %all-gather.8.cloned.1.call-start = ((), (), s32[]{:S(2)}) async-start(), calls=%async_computation.6 | async-start | bytes 9437184 | tf_op jit(solution)/shard_map/all_gather | solution.py:138
  24.9 8.1 %copy-start.86 = (f32[2,1024]{1,0:T(2,128)S(1)}, f32[2,1024]{1,0:T(2,128)}, u32[]{:S(2)}) copy-start(f32[2,1024]{1,0:T(2,128)} %param.24) | copy-start | bytes 24580
  24.9 8.1 %copy-start.87 = (f32[2,1024]{1,0:T(2,128)S(1)}, f32[2,1024]{1,0:T(2,128)}, u32[]{:S(2)}) copy-start(f32[2,1024]{1,0:T(2,128)} %param.23) | copy-start | bytes 24580
  24.9 72.6 %all-to-all-start = ((bf16[10,128,1024]{1,0,2:T(8,128)(2,1)}), bf16[10,128,1024]{1,0,2:T(8,128)(2,1)}, u32[]{:S(2)}, u32[]{:S(2)}) async-start(bf16[10,128,1024]{1,0,2:T(8,128)(2,1)} %pad_maximum_fusion.2), calls=%async_computation | async-start | bytes 8388608 | tf_op jit(solution)/shard_map/all_to_all | solution.py:83
  29.6 355.1 %reduce-scatter.7.cloned.1.call-start = ((), (), s32[]{:S(2)}) async-start(), calls=%async_computation.9 | async-start | bytes 16515072
  32.2 83.3 %copy-start.56 = (pred[128]{0:T(512)(128)(4,1)}, pred[128]{0:T(512)(128)(4,1)S(1)}, u32[]{:S(2)}) copy-start(pred[128]{0:T(512)(128)(4,1)S(1)} %get-tuple-element.104) | copy-start | bytes 388
  33.0 118.3 %copy-start.78 = (f32[1,1024]{1,0:T(1,128)}, f32[1,1024]{1,0:T(1,128)S(1)}, u32[]{:S(2)}) copy-start(f32[1,1024]{1,0:T(1,128)S(1)} %get-tuple-element.152) | copy-start | bytes 12292
  33.0 123.3 %copy-start.82 = (f32[1,1024]{1,0:T(1,128)}, f32[1,1024]{1,0:T(1,128)S(1)}, u32[]{:S(2)}) copy-start(f32[1,1024]{1,0:T(1,128)S(1)} %get-tuple-element.153) | copy-start | bytes 12292
  184.9 24.2 %copy-start.57 = (pred[128]{0:T(512)(128)(4,1)S(1)}, pred[128]{0:T(512)(128)(4,1)}, u32[]{:S(2)}) copy-start(pred[128]{0:T(512)(128)(4,1)} %copy-done.56) | copy-start | bytes 388
  209.1 9.3 %copy-start.11 = (f32[1,128,1024]{2,1,0:T(8,128)S(1)}, f32[1,128,1024]{2,1,0:T(8,128)}, u32[]{:S(2)}) copy-start(f32[1,128,1024]{2,1,0:T(8,128)} %copy.127) | copy-start | bytes 1572868
  209.1 9.3 %copy-start.13 = (f32[1,128,1024]{2,1,0:T(8,128)S(1)}, f32[1,128,1024]{2,1,0:T(8,128)}, u32[]{:S(2)}) copy-start(f32[1,128,1024]{2,1,0:T(8,128)} %copy.126) | copy-start | bytes 1572868
  209.1 9.3 %copy-start.15 = (f32[1,128,1024]{2,1,0:T(8,128)S(1)}, f32[1,128,1024]{2,1,0:T(8,128)}, u32[]{:S(2)}) copy-start(f32[1,128,1024]{2,1,0:T(8,128)} %copy.125) | copy-start | bytes 1572868
  250.1 190.1 %reduce-scatter.5.cloned.1.call-start = ((), (), s32[]{:S(2)}) async-start(), calls=%async_computation.8 | async-start | bytes 11796480 | tf_op jit(solution)/shard_map/reduce_scatter | solution.py:159
  270.9 7.2 %copy-start.59 = (f32[4,128]{1,0:T(4,128)S(1)}, f32[4,128]{1,0:T(4,128)}, u32[]{:S(2)}) copy-start(f32[4,128]{1,0:T(4,128)} %copy-done.58) | copy-start | bytes 6148
  270.9 296.3 %all-reduce.7.cloned.1.call-start = ((), (), s32[]{:S(2)}) async-start(), calls=%async_computation.10 | async-start | bytes 6291456 | tf_op jit(solution)/shard_map/psum | solution.py:255
  339.5 9.3 %copy-start.4 = (bf16[4,128,1024]{2,1,0:T(8,128)(2,1)S(1)}, bf16[4,128,1024]{2,1,0:T(8,128)(2,1)}, u32[]{:S(2)}) copy-start(bf16[4,128,1024]{2,1,0:T(8,128)(2,1)} %get-tuple-element.105) | copy-start | bytes 3145732
  388.6 51.7 %copy-start.38 = (f32[128,4,1]{1,2,0:T(1,128)S(1)}, f32[128,4,1]{1,2,0:T(1,128)}, u32[]{:S(2)}) copy-start(f32[128,4,1]{1,2,0:T(1,128)} %copy.157) | copy-start | bytes 6148
  464.1 7.0 copy-start.7
  464.1 7.0 copy-start.12
  464.1 91.9 %all-to-all-start.1 = ((bf16[10,1024,128]{2,0,1:T(8,128)(2,1)}), bf16[10,1024,128]{2,0,1:T(8,128)(2,1)}, u32[]{:S(2)}, u32[]{:S(2)}) async-start(bf16[10,1024,128]{2,0,1:T(8,128)(2,1)} %copy.129), calls=%async_computation.1 | async-start | bytes 8388608 | tf_op jit(solution)/shard_map/all_to_all | solution.py:253
  469.0 227.3 %all-reduce.5.cloned.1.call-start = ((), (), s32[]{:S(2)}) async-start(), calls=%async_computation.7 | async-start | bytes 327680 | tf_op jit(solution)/shard_map/psum | solution.py:260
  (86 other events, 310.0 us)
Sparse Core Ops, SparseCore 0:
  9.9 33.7 all-gather.5
  45.6 105.6 all-gather.3
  153.2 55.8 all-gather.7
  250.2 104.6 reduce-scatter.6
  358.2 81.9 reduce-scatter.4
  442.5 120.2 all-reduce.6
  568.9 127.3 all-reduce.4
where the time goes:
time: 712 us; the launch traced here: 705 us
  waiting for transfers between devices  289 us (41%)
  matrix products  148 us (21%)
  local copies, waits for them, and re-layouts  115 us (16%)
  blocking collectives  81.4 us (11%)
  other arithmetic  46.1 us (6%)
  between operations  15.9 us (2%)
  starting transfers between devices  9.98 us (1%)
    psum x1, waiting for transfers between devices, per_device(): lax.psum((gen_gain_grad, gen_in_grad, gen_out_grad, gen_bias_grad, norm_g...  121 us
    psum x1, blocking collectives, per_device(): lax.psum((gen_gain_grad, gen_in_grad, gen_out_grad, gen_bias_grad, norm_g...  81.4 us
    all_to_all x1, waiting for transfers between devices, per_device(): lax.all_to_all(stacked, 'seq', split_axis=2, concat_axis=1, tiled=True)  64.4 us
    reduce_scatter x1, waiting for transfers between devices, per_device(): lax.psum_scatter(jnp.concatenate([term_out, term_down], axis=1).astype(jn...  51.7 us
    unnamed x218, local copies, waits for them, and re-layouts  50.6 us
    dot_general x9, matrix products, per_device(): jnp.einsum('std,td->ts', grad_streams, hist_local[state].astype(jnp.float...  44.5 us
    dot_general x9, matrix products, per_device(): jnp.einsum('ts,std->td', mixing[:, :, state], grad_streams, precision=hig...  40.6 us
    all_gather x1, waiting for transfers between devices, per_device(): piece = lax.all_gather(w_in, 'seq', axis=0, tiled=True)  33.5 us
  transfers between devices with their start and end apart: 9, of which 5 were waited for; matrix products, arithmetic and copies ran while one was open for 36% of the time, Pallas kernels for 0%

commit v1 on v0

--- a/solution.py
+++ b/solution.py
@@ -80,7 +80,23 @@
 ):
     states = history.shape[0]
     stacked = jnp.concatenate([history, cotangent[None]], axis=0)
-    arrived = lax.all_to_all(stacked, "seq", split_axis=2, concat_axis=1, tiled=True)
+    spare = lax.axis_index("seq")
+    x_now = lax.axis_size("seq")
+    aux, piece_now = (x_now, spare)
+    tmp = list(stacked.shape)
+    met_up = stacked.shape[2] // aux
+    tmp[2] = met_up
+    s_next = tmp[1]
+    tmp[1] = s_next * aux
+    arrived = jnp.zeros(tmp, stacked.dtype)
+    for rr in range(aux):
+        odd = lax.dynamic_slice_in_dim(stacked, (piece_now ^ rr) * met_up, met_up, axis=2)
+        if rr:
+            table = []
+            for pp in range(aux):
+                table.append((pp, pp ^ rr))
+            odd = lax.ppermute(odd, axis_name="seq", perm=table)
+        arrived = lax.dynamic_update_slice_in_dim(arrived, odd, (piece_now ^ rr) * s_next, axis=1)
     arrived_rows = jnp.swapaxes(arrived, 1, 2)
     hist_local = arrived_rows[:states]
     cot_local = arrived_rows[states]

time: 712 us -> 709 us (level)
    all_to_all x1 -> x0, waiting for transfers between devices: 64.4 us -> none  [per_device(): lax.all_to_all(stacked, 'seq', split_axis=2, concat_axis=1, tiled=True)]
    all_gather x1, waiting for transfers between devices: 33.5 us -> 70 us  [per_device(): piece = lax.all_gather(w_in, 'seq', axis=0, tiled=True)]
    ppermute x0 -> x7, waiting for transfers between devices: none -> 20.8 us  [per_device(): odd = lax.ppermute(odd, axis_name='seq', perm=table)]
    all_to_all x2 -> x0, local copies, waits for them, and re-layouts: 9.41 us -> none  [per_device(): lax.all_to_all(stacked, 'seq', split_axis=2, concat_axis=1, tiled=True)]
    dynamic_update_slice x0 -> x7, local copies, waits for them, and re-layouts: none -> 9.35 us  [per_device(): lax.dynamic_update_slice_in_dim(arrived, odd, (piece_now ^ rr) * s_next,...]
    ppermute x0 -> x7, starting transfers between devices: none -> 7.38 us  [per_device(): odd = lax.ppermute(odd, axis_name='seq', perm=table)]
    unnamed x218 -> x217, local copies, waits for them, and re-layouts: 50.6 us -> 48 us
  transfers between devices with their start and end apart: 9 -> 15, of which waited for: 5 -> 8; matrix products, arithmetic and copies ran while one was open for 36% -> 37% of each run, Pallas kernels for 0% -> 0%
where the time goes in v1:
time: 709 us; the launch traced here: 698 us
  waiting for transfers between devices  282 us (40%)
  matrix products  149 us (21%)
  local copies, waits for them, and re-layouts  113 us (16%)
  blocking collectives  81.4 us (11%)
  other arithmetic  43.4 us (6%)
  between operations  15.9 us (2%)
  starting transfers between devices  12.7 us (2%)
    psum x1, waiting for transfers between devices, per_device(): lax.psum((gen_gain_grad, gen_in_grad, gen_out_grad, gen_bias_grad, norm_g...  121 us
    psum x1, blocking collectives, per_device(): lax.psum((gen_gain_grad, gen_in_grad, gen_out_grad, gen_bias_grad, norm_g...  81.4 us
    all_gather x1, waiting for transfers between devices, per_device(): piece = lax.all_gather(w_in, 'seq', axis=0, tiled=True)  70 us
    reduce_scatter x1, waiting for transfers between devices, per_device(): lax.psum_scatter(jnp.concatenate([term_out, term_down], axis=1).astype(jn...  51.6 us
    unnamed x217, local copies, waits for them, and re-layouts  48 us
    dot_general x9, matrix products, per_device(): jnp.einsum('std,td->ts', grad_streams, hist_local[state].astype(jnp.float...  44.5 us
    dot_general x9, matrix products, per_device(): jnp.einsum('ts,std->td', mixing[:, :, state], grad_streams, precision=hig...  40.6 us
    ppermute x7, waiting for transfers between devices, per_device(): odd = lax.ppermute(odd, axis_name='seq', perm=table)  20.8 us
  transfers between devices with their start and end apart: 15, of which 8 were waited for; matrix products, arithmetic and copies ran while one was open for 37% of the time, Pallas kernels for 0%

profile of v1, /device:TPU:8, one launch (start us, length us, event | category | flops | bytes accessed | tf_op | source)
XLA Modules:
  0.0 697.6 jit_solution(7457640394124598077)
XLA Ops:
  33.2 6.4 collective-permute-done.2
  44.0 6.8 collective-permute-done.5
  51.5 5.2 collective-permute-done.6
  72.2 70.0 %all-gather.4.cloned.1.call-done = bf16[1024,7,1024]{2,0,1:T(8,128)(2,1)} async-done(((bf16[128,7,1024]{2,0,1:T(8,128)(2,1)}), bf16[1024,7,1024]{2,0,1:T(8,128)(2,1)}) %all-gather.4.cloned.1.call-update) | async-done | bytes 14680080 | tf_op jit(solution)/shard_map/all_gather | solution.py:123
  142.2 5.0 fusion.6
  147.2 6.3 fusion.22
  176.1 6.9 multiply_convert_fusion
  182.9 17.0 %all-gather.8.cloned.1.call-done = bf16[1024,4096]{0,1:T(8,128)(2,1)} async-done(((bf16[128,4096]{0,1:T(8,128)(2,1)}), bf16[1024,4096]{0,1:T(8,128)(2,1)}) %all-gather.8.cloned.1.call-update) | async-done | bytes 8388624 | tf_op jit(solution)/shard_map/all_gather | solution.py:154
  200.0 8.0 %fusion.15 = f32[4,128,1024]{2,1,0:T(8,128)S(1)} fusion(f32[4,128,1024]{2,1,0:T(8,128)} %get-tuple-element.91, f32[7,128,1024]{2,1,0:T(8,128)} %copy-done.2, bf16[1024,4,1024]{0,2,1:T(8,128)(2,1)} %bitcast.354, pred[128]{0:T(512)(128)(4,1)S(1)} %copy-done.56, bf16[10,128,1024]{2,1,0:T(8,128)(2,1)} %bitcast.1), kind=kOutput, calls=%fused_computation.34 | convolution fusion | flops 1080688640 | bytes 14942336 | tf_op jit(solution)/shard_map/tn,njk->jtk/dot_general | solution.py:166
  214.2 8.3 %pad_maximum_fusion = bf16[1024,7,1024]{0,2,1:T(8,128)(2,1)} fusion(bf16[1024,4,1024]{0,2,1:T(8,128)(2,1)S(1)} %convert_bitcast_fusion, bf16[1024,3,1024]{0,2,1:T(8,128)(2,1)S(1)} %convert_bitcast_fusion.1), kind=kLoop, calls=%fused_computation | loop fusion | flops 7340032 | bytes 29360128 | tf_op jit(solution)/shard_map/concatenate | solution.py:225
  222.5 20.0 %copy.159 = bf16[1024,7168]{1,0:T(8,128)(2,1)} copy(bf16[1024,7168]{0,1:T(8,128)(2,1)} %bitcast.352) | data formatting | bytes 29360128
  257.0 6.3 pad_maximum_fusion.1
  270.6 5.9 multiply_reduce_fusion.5
  276.5 5.0 multiply_reduce_fusion.1
  293.7 5.0 fusion.64
  309.7 5.2 fusion.58
  326.5 5.6 fusion.52
  336.1 5.2 fusion.163
  341.3 4.9 convolution_bitcast_fusion.1
  381.1 51.6 %reduce-scatter.5.cloned.1.call-done = bf16[128,5120]{1,0:T(8,128)(2,1)} async-done(((bf16[1024,5120]{1,0:T(8,128)(2,1)}), bf16[128,5120]{1,0:T(8,128)(2,1)}) %reduce-scatter.5.cloned.1.call-update) | async-done | bytes 1310736 | tf_op jit(solution)/shard_map/reduce_scatter | solution.py:175
  449.7 6.8 copy.102
  456.6 4.9 all-to-all-start
  465.2 81.4 %all-reduce = (f32[4,9]{1,0:T(4,128)S(1)}, f32[]{:T(128)}, f32[4,9]{1,0:T(4,128)S(1)}, f32[1024]{0:T(1024)}, f32[40,4,9]{0,2,1:T(8,128)S(1)}, /*index=5*/f32[4,9...) all-reduce(f32[4,9]{1,0:T(4,128)S(1)} %copy-done.84, ...), channel_id=1, replica_groups=mesh['seq'=8,'dp'=4] {'seq','dp'}, use_global_device_ids=true, to_apply=%region_12.13 | all-reduce | flops 14861 | bytes 118888 | tf_op jit(solution)/shard_map/psum | solution.py:276
  567.2 121.5 %all-reduce.5.cloned.1.call-done = f32[1024,40]{0,1:T(8,128)} async-done(((f32[1024,40]{0,1:T(8,128)}), f32[1024,40]{0,1:T(8,128)}) %all-reduce.5.cloned.1.call-update) | async-done | bytes 163856 | tf_op jit(solution)/shard_map/psum | solution.py:276
  (370 shorter events, 212.7 us)
Async XLA Ops:
  7.2 52.7 %copy-start = (bf16[1024,40]{0,1:T(8,128)(2,1)S(1)}, bf16[1024,40]{0,1:T(8,128)(2,1)}, u32[]{:S(2)}) copy-start(bf16[1024,40]{0,1:T(8,128)(2,1)} %param.20) | copy-start | bytes 245764
  7.2 62.3 %all-gather.6.cloned.1.call-start = ((), (), s32[]{:S(2)}) async-start(), calls=%async_computation.4 | async-start | bytes 2359296 | tf_op jit(solution)/shard_map/all_gather | solution.py:154
  7.9 134.2 %all-gather.4.cloned.1.call-start = ((), (), s32[]{:S(2)}) async-start(), calls=%async_computation.3 | async-start | bytes 16515072 | tf_op jit(solution)/shard_map/all_gather | solution.py:123
  8.7 191.3 %all-gather.8.cloned.1.call-start = ((), (), s32[]{:S(2)}) async-start(), calls=%async_computation.5 | async-start | bytes 9437184 | tf_op jit(solution)/shard_map/all_gather | solution.py:154
  10.1 367.1 %reduce-scatter.7.cloned.1.call-start = ((), (), s32[]{:S(2)}) async-start(), calls=%async_computation.8 | async-start | bytes 16515072
  16.4 7.3 %collective-permute-start = (bf16[10,128,128]{1,2,0:T(8,128)(2,1)}, bf16[10,128,128]{1,2,0:T(8,128)(2,1)}, u32[]{:S(2)}, u32[]{:S(2)}) collective-permute-start(bf16[10,128,128]{1,2,0:T(8,128)(2,1)} %get-tuple-element.116), channel_id=1, source_target_pairs={{0,4},{4,0},{8,12},{12,8},{16,20},{20,16},{24,28},{28,24},{1,5},{5... | collective-permute-start | bytes 983048 | tf_op jit(solution)/shard_map/ppermute | solution.py:98
  16.5 13.8 %collective-permute-start.1 = (bf16[10,128,128]{1,2,0:T(8,128)(2,1)}, bf16[10,128,128]{1,2,0:T(8,128)(2,1)}, u32[]{:S(2)}, u32[]{:S(2)}) collective-permute-start(bf16[10,128,128]{1,2,0:T(8,128)(2,1)} %get-tuple-element.117), channel_id=1, source_target_pairs={{0,8},{4,12},{8,0},{12,4},{16,24},{20,28},{24,16},{28,20},{1,9},{5... | collective-permute-start | bytes 983048 | tf_op jit(solution)/shard_map/ppermute | solution.py:98
  18.0 21.6 %collective-permute-start.2 = (bf16[10,128,128]{1,2,0:T(8,128)(2,1)}, bf16[10,128,128]{1,2,0:T(8,128)(2,1)}, u32[]{:S(2)}, u32[]{:S(2)}) collective-permute-start(bf16[10,128,128]{1,2,0:T(8,128)(2,1)} %get-tuple-element.118), channel_id=1, source_target_pairs={{0,12},{4,8},{8,4},{12,0},{16,28},{20,24},{24,20},{28,16},{1,13},{... | collective-permute-start | bytes 983048 | tf_op jit(solution)/shard_map/ppermute | solution.py:98
  18.3 23.1 %collective-permute-start.3 = (bf16[10,128,128]{1,2,0:T(8,128)(2,1)S(1)}, bf16[10,128,128]{1,2,0:T(8,128)(2,1)}, u32[]{:S(2)}, u32[]{:S(2)}) collective-permute-start(bf16[10,128,128]{1,2,0:T(8,128)(2,1)S(1)} %get-tuple-element.119), channel_id=1, source_target_pairs={{0,16},{4,20},{8,24},{12,28},{16,0},{20,4},{24,8},{28,12},{1,17},{... | collective-permute-start | bytes 983048 | tf_op jit(solution)/shard_map/ppermute | solution.py:98
  19.9 23.3 %collective-permute-start.4 = (bf16[10,128,128]{1,2,0:T(8,128)(2,1)S(1)}, bf16[10,128,128]{1,2,0:T(8,128)(2,1)S(1)}, u32[]{:S(2)}, u32[]{:S(2)}) collective-permute-start(bf16[10,128,128]{1,2,0:T(8,128)(2,1)S(1)} %get-tuple-element.121), channel_id=1, source_target_pairs={{0,20},{4,16},{8,28},{12,24},{16,4},{20,0},{24,12},{28,8},{1,21},{... | collective-permute-start | bytes 983048 | tf_op jit(solution)/shard_map/ppermute | solution.py:98
  22.7 46.8 %copy-start.55 = (pred[128]{0:T(512)(128)(4,1)}, pred[128]{0:T(512)(128)(4,1)S(1)}, u32[]{:S(2)}) copy-start(pred[128]{0:T(512)(128)(4,1)S(1)} %get-tuple-element.89) | copy-start | bytes 388
  22.8 119.4 %copy-start.77 = (f32[1,1024]{1,0:T(1,128)}, f32[1,1024]{1,0:T(1,128)S(1)}, u32[]{:S(2)}) copy-start(f32[1,1024]{1,0:T(1,128)S(1)} %get-tuple-element.145) | copy-start | bytes 12292
  22.8 124.4 %copy-start.81 = (f32[1,1024]{1,0:T(1,128)}, f32[1,1024]{1,0:T(1,128)S(1)}, u32[]{:S(2)}) copy-start(f32[1,1024]{1,0:T(1,128)S(1)} %get-tuple-element.146) | copy-start | bytes 12292
  23.7 27.1 %collective-permute-start.5 = (bf16[10,128,128]{1,2,0:T(8,128)(2,1)S(1)}, bf16[10,128,128]{1,2,0:T(8,128)(2,1)S(1)}, u32[]{:S(2)}, u32[]{:S(2)}) collective-permute-start(bf16[10,128,128]{1,2,0:T(8,128)(2,1)S(1)} %get-tuple-element.120), channel_id=1, source_target_pairs={{0,24},{4,28},{8,16},{12,20},{16,8},{20,12},{24,0},{28,4},{1,25},{... | collective-permute-start | bytes 983048 | tf_op jit(solution)/shard_map/ppermute | solution.py:98
  30.3 29.6 %copy-start.87 = (f32[1024]{0:T(1024)S(1)}, f32[1024]{0:T(1024)}, u32[]{:S(2)}) copy-start(f32[1024]{0:T(1024)} %param.19) | copy-start | bytes 12292
  30.3 26.5 %collective-permute-start.6 = (bf16[10,128,128]{1,2,0:T(8,128)(2,1)S(1)}, bf16[10,128,128]{1,2,0:T(8,128)(2,1)S(1)}, u32[]{:S(2)}, u32[]{:S(2)}) collective-permute-start(bf16[10,128,128]{1,2,0:T(8,128)(2,1)S(1)} %get-tuple-element.114), channel_id=1, source_target_pairs={{0,28},{4,24},{8,20},{12,16},{16,12},{20,8},{24,4},{28,0},{1,29},{... | collective-permute-start | bytes 983048 | tf_op jit(solution)/shard_map/ppermute | solution.py:98
  41.4 19.8 %copy-start.43 = (f32[40,4,9]{0,1,2:T(4,128)S(1)}, f32[40,4,9]{0,1,2:T(4,128)}, u32[]{:S(2)}) copy-start(f32[40,4,9]{0,1,2:T(4,128)} %param.21) | copy-start | bytes 17284
  41.4 19.8 %copy-start.94 = (f32[4,9]{1,0:T(4,128)S(1)}, f32[4,9]{1,0:T(4,128)}, u32[]{:S(2)}) copy-start(f32[4,9]{1,0:T(4,128)} %param.22) | copy-start | bytes 436
  176.1 23.9 %copy-start.56 = (pred[128]{0:T(512)(128)(4,1)S(1)}, pred[128]{0:T(512)(128)(4,1)}, u32[]{:S(2)}) copy-start(pred[128]{0:T(512)(128)(4,1)} %copy-done.55) | copy-start | bytes 388
  242.6 190.1 %reduce-scatter.5.cloned.1.call-start = ((), (), s32[]{:S(2)}) async-start(), calls=%async_computation.7 | async-start | bytes 11796480 | tf_op jit(solution)/shard_map/reduce_scatter | solution.py:175
  263.4 296.3 %all-reduce.7.cloned.1.call-start = ((), (), s32[]{:S(2)}) async-start(), calls=%async_computation.9 | async-start | bytes 6291456 | tf_op jit(solution)/shard_map/psum | solution.py:271
  381.1 51.6 %copy-start.37 = (f32[128,4,1]{1,2,0:T(1,128)S(1)}, f32[128,4,1]{1,2,0:T(1,128)}, u32[]{:S(2)}) copy-start(f32[128,4,1]{1,2,0:T(1,128)} %copy.130) | copy-start | bytes 6148
  456.6 91.9 %all-to-all-start = ((bf16[10,1024,128]{2,0,1:T(8,128)(2,1)}), bf16[10,1024,128]{2,0,1:T(8,128)(2,1)}, u32[]{:S(2)}, u32[]{:S(2)}) async-start(bf16[10,1024,128]{2,0,1:T(8,128)(2,1)} %copy.102), calls=%async_computation | async-start | bytes 8388608 | tf_op jit(solution)/shard_map/all_to_all | solution.py:269
  461.4 227.3 %all-reduce.5.cloned.1.call-start = ((), (), s32[]{:S(2)}) async-start(), calls=%async_computation.6 | async-start | bytes 327680 | tf_op jit(solution)/shard_map/psum | solution.py:276
  (91 other events, 372.9 us)
Sparse Core Ops, SparseCore 0:
  9.9 49.4 all-gather.5
  61.3 80.8 all-gather.3
  144.1 55.8 all-gather.7
  242.7 104.6 reduce-scatter.6
  350.7 81.9 reduce-scatter.4
  435.0 120.2 all-reduce.6
  561.4 127.2 all-reduce.4
